TPU v7x, 256 devices: a whole 4x4x8 slice. The times are simulated.
256 devices in a mesh: coil: 32 (over z, y), slab: 8 (over x, core).
Axes of the slice: x: 4, y: 4, z: 8, core: 2. Of those that a mesh axis runs over, the one named last changes fastest.
Arguments:
- cotangent: float32 [32, 2, 256, 256], P('coil', None, 'slab'), may hold values from -60 to 60
- saved_solution: float32 [32, 2, 256, 256], P('coil', None, 'slab'), may hold values from -6 to 6
- coil_maps: bfloat16 [32, 32, 2, 256, 256], P('coil', None, None, 'slab'), may hold values from -1.5 to 1.5
- kspace: bfloat16 [32, 32, 2, 256, 256], P('coil', None, None, 'slab'), may hold values from -6 to 6
- mask_logit: float32 [32, 256], P(None, 'slab'), may hold values from -4.5 to 4.5
- reach: int32 [32, 256], P(None, 'slab'), may hold values from 0 to 256, as said below
Outputs:
- image_grad: float32 [32, 2, 256, 256], P('coil', None, 'slab')
- kspace_grad: bfloat16 [32, 32, 2, 256, 256], P('coil', None, None, 'slab')
- logit_grad: float32 [32, 256], P(None, 'slab')
Inputs may be any that keep to these rules, and one draw needn't show every extreme that they name: reach[z, y] is 0 (line not acquired) or between 128 and 256; line [0, 0] is always fully acquired and line [0, 128] never.
All inputs are finite; a program needn't handle non-finite values.
Results may differ from a plain program's by a relative error of at most 0.02.
Values may be sent and summed in bfloat16 or wider, within the bound.
A program may use at most 64 MiB of HBM per device.

v0:
```python
import math
import jax
import jax.numpy as jnp
from jax import lax
from jax.sharding import PartitionSpec as P

NX = 256
NY = 256
NZ = 32
ITERS = 2
DAMPING = 0.2


def dft_table(length, sign):
    index = jnp.arange(length, dtype=jnp.int32)
    phase = (index[:, None] * index[None, :] % length).astype(jnp.float32) * (
        2.0 * math.pi / length
    )
    factor = 1.0 / math.sqrt(length)
    cosine = jnp.cos(phase) * factor
    sine = sign * jnp.sin(phase) * factor
    table = jnp.stack(
        [jnp.stack([cosine, sine], axis=1), jnp.stack([-sine, cosine], axis=1)], axis=0
    )
    return table.astype(jnp.bfloat16)


def complex_product(factor, operand):
    factor_re, factor_im = (factor[:, 0], factor[:, 1])
    operand_re, operand_im = (operand[:, 0], operand[:, 1])
    return jnp.stack(
        [
            factor_re * operand_re - factor_im * operand_im,
            factor_re * operand_im + factor_im * operand_re,
        ],
        axis=1,
    )


def conjugate_product(factor, operand):
    factor_re, factor_im = (factor[:, 0], factor[:, 1])
    operand_re, operand_im = (operand[:, 0], operand[:, 1])
    return jnp.stack(
        [
            factor_re * operand_re + factor_im * operand_im,
            factor_re * operand_im - factor_im * operand_re,
        ],
        axis=1,
    )


def shards(cotangent, saved_solution, coil_maps, kspace, mask_logit, reach):
    y_fwd, y_inv = (dft_table(NY, -1.0), dft_table(NY, 1.0))
    z_fwd, z_inv = (dft_table(NZ, -1.0), dft_table(NZ, 1.0))
    x_fwd, x_inv = (dft_table(NX, -1.0), dft_table(NX, 1.0))
    maps = coil_maps[0]
    data = kspace[0].astype(jnp.float32)
    readout = jnp.arange(NX, dtype=jnp.int32)
    centred = (readout + NX // 2) % NX
    sampled = (centred[None, None, :] >= (NX - reach)[:, :, None]).astype(jnp.float32)
    gate = jax.nn.sigmoid(mask_logit)
    weight = sampled * gate[:, :, None]
    squared = (weight * weight)[:, None]

    def front(piece):
        product = complex_product(maps.astype(jnp.float32), piece.astype(jnp.float32)).astype(
            jnp.bfloat16
        )
        return jnp.einsum(
            "zixn,inok->zoxk", product, y_fwd, preferred_element_type=jnp.float32
        ).astype(jnp.bfloat16)

    def gathered_front(shard):
        return front(lax.all_gather(shard, "coil", axis=0, tiled=True))

    def to_kspace(rows):
        mixed = jnp.einsum(
            "nixk,inom->moxk", rows, z_fwd, preferred_element_type=jnp.float32
        ).astype(jnp.bfloat16)
        swapped = lax.all_to_all(mixed, "slab", split_axis=3, concat_axis=2, tiled=True)
        return jnp.einsum("zink,inoq->zokq", swapped, x_fwd, preferred_element_type=jnp.float32)

    direction = cotangent
    both = ("coil", "slab")
    saved_k = to_kspace(gathered_front(saved_solution.astype(jnp.bfloat16)))
    first_k = to_kspace(gathered_front(direction.astype(jnp.bfloat16)))
    first_w = weight[:, None] * first_k
    norm_now, first_energy = lax.psum(
        (jnp.sum(direction * direction), jnp.sum(first_w * first_w)), both
    )
    apply_spectrum = (squared * first_k).astype(jnp.bfloat16)
    to_mixed = jnp.einsum(
        "zikq,iqon->zonk", apply_spectrum, x_inv, preferred_element_type=jnp.float32
    ).astype(jnp.bfloat16)
    to_swapped = lax.all_to_all(to_mixed, "slab", split_axis=2, concat_axis=3, tiled=True)
    apply_image_rows = jnp.einsum(
        "mixk,imon->noxk", to_swapped, z_inv, preferred_element_type=jnp.float32
    ).astype(jnp.bfloat16)
    image = jnp.einsum(
        "zixk,ikon->zoxn", apply_image_rows, y_inv, preferred_element_type=jnp.float32
    )
    summed = lax.psum_scatter(
        conjugate_product(maps.astype(jnp.float32), image).astype(jnp.bfloat16),
        "coil",
        scatter_dimension=0,
        tiled=True,
    ).astype(jnp.float32)
    image = summed + DAMPING * direction
    alpha = norm_now / (first_energy + DAMPING * norm_now)
    residual = direction - alpha * image
    second_k = to_kspace(gathered_front(residual.astype(jnp.bfloat16)))
    second_w = weight[:, None] * second_k
    gain = gate * (1.0 - gate)
    target = data - 2.0 * weight[:, None] * saved_k

    def line_terms(spectrum):
        return gain * jnp.sum(sampled * jnp.sum(spectrum * target, axis=1), axis=2)

    norm_next, crossing, second_energy, mixed_energy = lax.psum(
        (
            jnp.sum(residual * residual),
            jnp.sum(residual * direction),
            jnp.sum(second_w * second_w),
            jnp.sum(second_w * first_w),
        ),
        both,
    )
    lines = lax.psum(jnp.stack([line_terms(first_k), line_terms(second_k)]), "coil")
    beta = norm_next / norm_now
    curvature = (
        second_energy
        + beta * (2.0 * mixed_energy + beta * first_energy)
        + DAMPING * (norm_next + beta * (2.0 * crossing + beta * norm_now))
    )
    later = norm_next / curvature
    early = alpha + later * beta
    image_grad = DAMPING * (early * direction + later * residual)
    kspace_grad = (early * first_w + later * second_w).astype(jnp.bfloat16)[None]
    logit_grad = early * lines[0] + later * lines[1]
    return (image_grad, kspace_grad, logit_grad)


def solution(mesh):
    placed = (
        P("coil", None, "slab", None),
        P("coil", None, "slab", None),
        P("coil", None, None, "slab", None),
        P("coil", None, None, "slab", None),
        P(None, "slab"),
        P(None, "slab"),
    )
    return jax.shard_map(
        shards,
        mesh=mesh,
        in_specs=placed,
        out_specs=(
            P("coil", None, "slab", None),
            P("coil", None, None, "slab", None),
            P(None, "slab"),
        ),
        check_vma=False,
    )
```

profile of v0, /device:TPU:2, one launch (start us, length us, event | category | flops | bytes accessed | tf_op | source)
XLA Modules:
  0.0 753.5 jit_solution(7913596652548034315)
XLA Ops:
  7.2 2.1 fusion.89
  14.3 1.8 bitcast_convert_fusion.8
  16.2 74.3 %all-gather.4.cloned.1.call-done = bf16[32,2,32,256]{3,2,1,0:T(8,128)(2,1)} async-done(((bf16[1,2,32,256]{3,2,1,0:T(8,128)(2,1)}), bf16[32,2,32,256]{3,2,1,0:T(8,128)(2,1)}) %all-gather.4.cloned.1.call-update) | async-done | bytes 1048592 | tf_op jit(solution)/shard_map/all_gather | solution.py:74
  90.6 1.8 copy_convert_fusion.2
  93.9 3.2 fusion.4
  97.1 7.2 copy.81
  104.3 7.8 %reshape.272 = bf16[8,2,32768]{2,1,0:T(2,128)(2,1)} reshape(bf16[256,2,32,32]{3,2,1,0:T(8,128)(2,1)} %bitcast.296) | data formatting | bytes 2097152
  112.2 5.5 all-to-all-start
  120.4 11.7 %all-to-all-done = bf16[8,2,32768]{2,1,0:T(2,128)(2,1)} async-done(((bf16[8,2,32768]{2,1,0:T(2,128)(2,1)}), bf16[8,2,32768]{2,1,0:T(2,128)(2,1)}, u32[]{:S(2)}, u32[]{:S(2)}) %all-to-all-start) | async-done | bytes 1048608 | tf_op jit(solution)/shard_map/all_to_all | solution.py:80
  132.1 7.0 reshape.273
  139.1 6.7 copy.82
  145.9 6.2 reshape.243
  152.0 4.4 fusion.2
  158.1 7.2 copy.85
  165.3 7.8 %reshape.274 = bf16[8,2,32768]{2,1,0:T(2,128)(2,1)} reshape(bf16[256,2,32,32]{3,2,1,0:T(8,128)(2,1)} %bitcast.297) | data formatting | bytes 2097152
  173.2 5.6 all-to-all-start.1
  178.9 3.2 copy_convert_fusion
  182.1 11.2 %all-to-all-done.1 = bf16[8,2,32768]{2,1,0:T(2,128)(2,1)} async-done(((bf16[8,2,32768]{2,1,0:T(2,128)(2,1)}), bf16[8,2,32768]{2,1,0:T(2,128)(2,1)}, u32[]{:S(2)}, u32[]{:S(2)}) %all-to-all-start.1) | async-done | bytes 1048608 | tf_op jit(solution)/shard_map/all_to_all | solution.py:95
  193.3 7.0 reshape.275
  200.4 6.9 copy.160
  207.2 6.2 all_to_all.59
  213.4 2.2 fusion.5
  217.2 1.9 subtract_convert_fusion
  221.5 73.8 %all-reduce.2 = (f32[]{:T(128)}, f32[]{:T(128)}) all-reduce(f32[]{:T(128)} %get-tuple-element.49, f32[]{:T(128)} %get-tuple-element.40), channel_id=1, replica_groups=mesh['coil'=32,'slab'=8] {'coil','slab'}, use_global_device_ids=true, to_apply=%region_1.2 | all-reduce | flops 2 | bytes 16 | tf_op jit(solution)/shard_map/psum | solution.py:88
  297.2 71.0 %all-reduce.5.cloned.1.call-done = bf16[32,2,32,256]{3,2,0,1:T(8,128)(2,1)} async-done(((bf16[32,2,32,256]{3,2,0,1:T(8,128)(2,1)}), bf16[32,2,32,256]{3,2,0,1:T(8,128)(2,1)}) %all-reduce.5.cloned.1.call-update) | async-done | bytes 1048592
  368.2 2.7 fusion.61
  370.9 3.3 fusion.7
  374.1 7.2 copy.103
  381.4 7.8 %reshape.278 = bf16[8,2,32768]{2,1,0:T(2,128)(2,1)} reshape(bf16[256,2,32,32]{3,2,1,0:T(8,128)(2,1)} %bitcast.298) | data formatting | bytes 2097152
  389.2 5.1 all-to-all-start.3
  394.3 50.5 %all-gather.6.cloned.1.call-done = bf16[32,2,32,256]{3,2,1,0:T(8,128)(2,1)} async-done(((bf16[1,2,32,256]{3,2,1,0:T(8,128)(2,1)}), bf16[32,2,32,256]{3,2,1,0:T(8,128)(2,1)}) %all-gather.6.cloned.1.call-update) | async-done | bytes 1048592 | tf_op jit(solution)/shard_map/all_gather | solution.py:74
  448.2 2.3 fusion.6
  450.5 6.5 copy.97
  457.0 7.8 %reshape.276 = bf16[8,2,32768]{2,1,0:T(2,128)(2,1)} reshape(bf16[256,2,32,32]{3,2,1,0:T(8,128)(2,1)} %bitcast.299) | data formatting | bytes 2097152
  464.8 4.8 all-to-all-start.2
  469.6 7.0 reshape.279
  476.6 6.7 copy.104
  483.3 5.4 reshape.264
  488.7 3.4 fusion
  492.1 7.0 reshape.277
  499.1 6.7 copy.98
  505.8 6.3 reshape.258
  512.1 6.2 multiply_reduce_fusion
  518.3 74.5 %all-reduce.1 = (f32[]{:T(128)}, f32[]{:T(128)}, f32[]{:T(128)}, f32[]{:T(128)}) all-reduce(f32[]{:T(128)} %get-tuple-element.20, f32[]{:T(128)} %get-tuple-element.16, f32[]{:T(128)} %get-tuple-element.15, f32[]{:T(128)} %get-tuple-element.19), channel_id=1, replica_groups=mesh['coil'=32,'slab'=8] {'coil','slab'}, use_global_device_ids=true, to_apply=%region_6.7 | all-reduce | flops 4 | bytes 32 | tf_op jit(solution)/shard_map/psum | solution.py:119
  595.3 2.1 fusion.12
  597.4 140.0 %psum.55 = f32[2,32,32]{2,1,0:T(8,128)S(1)} all-reduce(f32[2,32,32]{2,1,0:T(8,128)S(1)} %pad_maximum_fusion.7), channel_id=1, replica_groups=mesh['coil'=32,'slab'=8] {'coil'}, use_global_device_ids=true, to_apply=%region_17.18 | all-reduce | flops 2048 | bytes 16384 | tf_op jit(solution)/shard_map/psum | solution.py:128
  741.3 2.3 fusion.14
  744.7 2.0 fusion.64
  (57 shorter events, 20.2 us)
Async XLA Ops:
  7.2 83.4 %all-gather.4.cloned.1.call-start = ((), (), s32[]{:S(2)}) async-start(), calls=%async_computation.4 | async-start | bytes 1081344 | tf_op jit(solution)/shard_map/all_gather | solution.py:74
  9.4 169.6 %all-gather.8.cloned.1.call-start = ((), (), s32[]{:S(2)}) async-start(), calls=%async_computation.6 | async-start | bytes 1081344 | tf_op jit(solution)/shard_map/all_gather | solution.py:74
  16.2 77.7 %copy-start.3 = (bf16[1,256,2,256]{3,1,0,2:T(8,128)(2,1)}, bf16[1,256,2,256]{3,1,0,2:T(8,128)(2,1)S(1)}, u32[]{:S(2)}) copy-start(bf16[1,256,2,256]{3,1,0,2:T(8,128)(2,1)S(1)} %get-tuple-element.47) | copy-start | bytes 786436
  112.1 6.5 copy-start.8
  112.2 6.6 copy-start.7
  112.2 20.0 %all-to-all-start = ((bf16[8,2,32768]{2,1,0:T(2,128)(2,1)}), bf16[8,2,32768]{2,1,0:T(2,128)(2,1)}, u32[]{:S(2)}, u32[]{:S(2)}) async-start(bf16[8,2,32768]{2,1,0:T(2,128)(2,1)} %reshape.272), calls=%async_computation | async-start | bytes 2097152 | tf_op jit(solution)/shard_map/all_to_all | solution.py:80
  152.0 4.4 copy-start.6
  173.2 20.2 %all-to-all-start.1 = ((bf16[8,2,32768]{2,1,0:T(2,128)(2,1)}), bf16[8,2,32768]{2,1,0:T(2,128)(2,1)}, u32[]{:S(2)}, u32[]{:S(2)}) async-start(bf16[8,2,32768]{2,1,0:T(2,128)(2,1)} %reshape.274), calls=%async_computation.1 | async-start | bytes 2097152 | tf_op jit(solution)/shard_map/all_to_all | solution.py:95
  178.7 189.4 %all-reduce.5.cloned.1.call-start = ((), (), s32[]{:S(2)}) async-start(), calls=%async_computation.7 | async-start | bytes 2097152
  213.4 2.2 copy-start.5
  215.6 1.6 copy-start.1
  219.2 1.7 copy-start.9
  219.2 148.9 %copy-start.4 = (f32[1,2,32,256]{3,2,1,0:T(8,128)S(1)}, f32[1,2,32,256]{3,2,1,0:T(8,128)}, u32[]{:S(2)}) copy-start(f32[1,2,32,256]{3,2,1,0:T(8,128)} %param.6) | copy-start | bytes 196612
  220.8 224.0 %all-gather.6.cloned.1.call-start = ((), (), s32[]{:S(2)}) async-start(), calls=%async_computation.5 | async-start | bytes 1081344 | tf_op jit(solution)/shard_map/all_gather | solution.py:74
  389.2 75.6 %all-to-all-start.3 = ((bf16[8,2,32768]{2,1,0:T(2,128)(2,1)}), bf16[8,2,32768]{2,1,0:T(2,128)(2,1)}, u32[]{:S(2)}, u32[]{:S(2)}) async-start(bf16[8,2,32768]{2,1,0:T(2,128)(2,1)} %reshape.278), calls=%async_computation.3 | async-start | bytes 2097152 | tf_op jit(solution)/shard_map/all_to_all | solution.py:80
  464.8 27.3 %all-to-all-start.2 = ((bf16[8,2,32768]{2,1,0:T(2,128)(2,1)}), bf16[8,2,32768]{2,1,0:T(2,128)(2,1)}, u32[]{:S(2)}, u32[]{:S(2)}) async-start(bf16[8,2,32768]{2,1,0:T(2,128)(2,1)} %reshape.276), calls=%async_computation.2 | async-start | bytes 2097152 | tf_op jit(solution)/shard_map/all_to_all | solution.py:80
  483.3 5.4 copy-start.2
  505.8 6.3 copy-start
Sparse Core Ops, SparseCore 0:
  11.1 79.3 all-gather.3
  93.1 73.8 all-gather.7
  221.0 147.1 all-reduce.4
  371.2 73.5 all-gather.5
where the time goes:
time: 763 us; the launch traced here: 753 us
  blocking collectives  288 us (38%)
  waiting for transfers between devices  219 us (29%)
  local copies, waits for them, and re-layouts  143 us (19%)
  other arithmetic  33.3 us (4%)
  matrix products  27.2 us (4%)
  between operations  21.9 us (3%)
  starting transfers between devices  21.2 us (3%)
    psum x1, blocking collectives, shards(): lax.psum(jnp.stack([line_terms(first_k), line_terms(second_k)]), 'coil')  140 us
    all_gather x3, waiting for transfers between devices, gathered_front(): return front(lax.all_gather(shard, 'coil', axis=0, tiled=True))  125 us
    psum x1, blocking collectives, shards(): lax.psum((jnp.sum(residual * residual), jnp.sum(residual * direction), jn...  74.5 us
    psum x1, blocking collectives, shards(): lax.psum((jnp.sum(direction * direction), jnp.sum(first_w * first_w)), both)  73.8 us
    unnamed x5, waiting for transfers between devices  71.1 us
    unnamed x30, local copies, waits for them, and re-layouts  61.8 us
    all_to_all x6, local copies, waits for them, and re-layouts, to_kspace(): lax.all_to_all(mixed, 'slab', split_axis=3, concat_axis=2, tiled=True)  38 us
    convert_element_type x3, local copies, waits for them, and re-layouts, to_kspace(): mixed = jnp.einsum('nixk,inom->moxk', rows, z_fwd, preferred_element_type...  21 us
  transfers between devices with their start and end apart: 8, of which 5 were waited for; matrix products, arithmetic and copies ran while one was open for 18% of the time, Pallas kernels for 0%

commit v1 on v0

--- a/solution.py
+++ b/solution.py
@@ -125,7 +125,9 @@
         ),
         both,
     )
-    lines = lax.psum(jnp.stack([line_terms(first_k), line_terms(second_k)]), "coil")
+    x = jnp.stack([line_terms(first_k), line_terms(second_k)])
+    shards_2 = lax.all_gather(x, "coil")
+    lines = jnp.sum(shards_2, axis=0)
     beta = norm_next / norm_now
     curvature = (
         second_energy

time: 763 us -> 677 us (0.89)
  blocking collectives: 288 us -> 201 us
    psum x1 -> x0, blocking collectives: 140 us -> none  [shards(): lax.psum(jnp.stack([line_terms(first_k), line_terms(second_k)]), 'coil')]
    all_gather x0 -> x1, blocking collectives: none -> 53.1 us  [shards(): shards_2 = lax.all_gather(x, 'coil')]
  transfers between devices with their start and end apart: 8 -> 8, of which waited for: 5 -> 5; matrix products, arithmetic and copies ran while one was open for 18% -> 20% of each run, Pallas kernels for 0% -> 0%
where the time goes in v1:
time: 677 us; the launch traced here: 668 us
  waiting for transfers between devices  219 us (32%)
  blocking collectives  201 us (30%)
  local copies, waits for them, and re-layouts  143 us (21%)
  other arithmetic  34.6 us (5%)
  matrix products  27.2 us (4%)
  between operations  21.9 us (3%)
  starting transfers between devices  21.2 us (3%)
    all_gather x3, waiting for transfers between devices, gathered_front(): return front(lax.all_gather(shard, 'coil', axis=0, tiled=True))  125 us
    psum x1, blocking collectives, shards(): lax.psum((jnp.sum(residual * residual), jnp.sum(residual * direction), jn...  74.5 us
    psum x1, blocking collectives, shards(): lax.psum((jnp.sum(direction * direction), jnp.sum(first_w * first_w)), both)  73.8 us
    unnamed x5, waiting for transfers between devices  71.1 us
    unnamed x30, local copies, waits for them, and re-layouts  61.8 us
    all_gather x1, blocking collectives, shards(): shards_2 = lax.all_gather(x, 'coil')  53.1 us
    all_to_all x6, local copies, waits for them, and re-layouts, to_kspace(): lax.all_to_all(mixed, 'slab', split_axis=3, concat_axis=2, tiled=True)  38 us
    convert_element_type x3, local copies, waits for them, and re-layouts, to_kspace(): mixed = jnp.einsum('nixk,inom->moxk', rows, z_fwd, preferred_element_type...  21 us
  transfers between devices with their start and end apart: 8, of which 5 were waited for; matrix products, arithmetic and copies ran while one was open for 20% of the time, Pallas kernels for 0%

profile of v1, /device:TPU:2, one launch (start us, length us, event | category | flops | bytes accessed | tf_op | source)
XLA Modules:
  0.0 667.9 jit_solution(2360762838258197628)
XLA Ops:
  7.2 2.1 fusion.89
  14.3 1.8 bitcast_convert_fusion.8
  16.2 74.3 %all-gather.5.cloned.1.call-done = bf16[32,2,32,256]{3,2,1,0:T(8,128)(2,1)} async-done(((bf16[1,2,32,256]{3,2,1,0:T(8,128)(2,1)}), bf16[32,2,32,256]{3,2,1,0:T(8,128)(2,1)}) %all-gather.5.cloned.1.call-update) | async-done | bytes 1048592 | tf_op jit(solution)/shard_map/all_gather | solution.py:74
  90.6 1.8 copy_convert_fusion.2
  93.9 3.2 fusion.4
  97.1 7.2 %copy.81 = bf16[32,2,32,256]{0,2,1,3:T(8,128)(2,1)} copy(bf16[32,2,32,256]{3,0,2,1:T(8,128)(2,1)} %fusion.4) | data formatting | bytes 2097152 | tf_op jit(solution)/shard_map/convert_element_type | solution.py:79
  104.3 7.8 %reshape.273 = bf16[8,2,32768]{2,1,0:T(2,128)(2,1)} reshape(bf16[256,2,32,32]{3,2,1,0:T(8,128)(2,1)} %bitcast.297) | data formatting | bytes 2097152
  112.2 5.5 all-to-all-start
  120.4 11.7 %all-to-all-done = bf16[8,2,32768]{2,1,0:T(2,128)(2,1)} async-done(((bf16[8,2,32768]{2,1,0:T(2,128)(2,1)}), bf16[8,2,32768]{2,1,0:T(2,128)(2,1)}, u32[]{:S(2)}, u32[]{:S(2)}) %all-to-all-start) | async-done | bytes 1048608 | tf_op jit(solution)/shard_map/all_to_all | solution.py:80
  132.1 7.0 %reshape.274 = bf16[256,2,32,32]{3,2,1,0:T(8,128)(2,1)} reshape(bf16[8,2,32768]{2,1,0:T(2,128)(2,1)} %all-to-all-done) | data formatting | bytes 2097152
  139.1 6.7 %copy.82 = bf16[32,2,32,8,32]{2,3,4,1,0:T(8,128)(2,1)} copy(bf16[32,2,32,8,32]{0,2,1,4,3:T(8,128)(2,1)} %bitcast.301) | data formatting | bytes 2097152 | tf_op jit(solution)/shard_map/all_to_all | solution.py:80
  145.9 6.2 reshape.244
  152.0 4.4 fusion.2
  158.1 7.2 %copy.85 = bf16[32,2,256,32]{3,0,1,2:T(8,128)(2,1)} copy(bf16[32,2,256,32]{2,3,0,1:T(8,128)(2,1)} %fusion.9) | data formatting | bytes 2097152 | tf_op jit(solution)/shard_map/convert_element_type | solution.py:94
  165.3 7.8 %reshape.275 = bf16[8,2,32768]{2,1,0:T(2,128)(2,1)} reshape(bf16[256,2,32,32]{3,2,1,0:T(8,128)(2,1)} %bitcast.298) | data formatting | bytes 2097152
  173.2 5.6 all-to-all-start.1
  178.9 3.2 copy_convert_fusion
  182.1 11.2 %all-to-all-done.1 = bf16[8,2,32768]{2,1,0:T(2,128)(2,1)} async-done(((bf16[8,2,32768]{2,1,0:T(2,128)(2,1)}), bf16[8,2,32768]{2,1,0:T(2,128)(2,1)}, u32[]{:S(2)}, u32[]{:S(2)}) %all-to-all-start.1) | async-done | bytes 1048608 | tf_op jit(solution)/shard_map/all_to_all | solution.py:95
  193.3 7.0 %reshape.276 = bf16[256,2,32,32]{3,2,1,0:T(8,128)(2,1)} reshape(bf16[8,2,32768]{2,1,0:T(2,128)(2,1)} %all-to-all-done.1) | data formatting | bytes 2097152
  200.4 6.9 %copy.160 = bf16[32,2,8,32,32]{4,2,3,1,0:T(8,128)(2,1)} copy(bf16[32,2,8,32,32]{4,0,1,3,2:T(8,128)(2,1)} %bitcast.303) | data formatting | bytes 2097152 | tf_op jit(solution)/shard_map/all_to_all | solution.py:95
  207.2 6.2 all_to_all.59
  213.4 2.2 fusion.5
  217.2 1.9 subtract_convert_fusion
  221.5 73.8 %all-reduce.2 = (f32[]{:T(128)}, f32[]{:T(128)}) all-reduce(f32[]{:T(128)} %get-tuple-element.49, f32[]{:T(128)} %get-tuple-element.40), channel_id=1, replica_groups=mesh['coil'=32,'slab'=8] {'coil','slab'}, use_global_device_ids=true, to_apply=%region_1.2 | all-reduce | flops 2 | bytes 16 | tf_op jit(solution)/shard_map/psum | solution.py:88
  297.2 71.0 %all-reduce.5.cloned.1.call-done = bf16[32,2,32,256]{3,2,0,1:T(8,128)(2,1)} async-done(((bf16[32,2,32,256]{3,2,0,1:T(8,128)(2,1)}), bf16[32,2,32,256]{3,2,0,1:T(8,128)(2,1)}) %all-reduce.5.cloned.1.call-update) | async-done | bytes 1048592
  368.2 2.7 fusion.61
  370.9 3.3 fusion.7
  374.1 7.2 %copy.103 = bf16[32,2,32,256]{0,2,1,3:T(8,128)(2,1)} copy(bf16[32,2,32,256]{3,0,2,1:T(8,128)(2,1)} %fusion.7) | data formatting | bytes 2097152 | tf_op jit(solution)/shard_map/convert_element_type | solution.py:79
  381.4 7.8 %reshape.279 = bf16[8,2,32768]{2,1,0:T(2,128)(2,1)} reshape(bf16[256,2,32,32]{3,2,1,0:T(8,128)(2,1)} %bitcast.299) | data formatting | bytes 2097152
  389.2 5.1 all-to-all-start.3
  394.3 50.5 %all-gather.7.cloned.1.call-done = bf16[32,2,32,256]{3,2,1,0:T(8,128)(2,1)} async-done(((bf16[1,2,32,256]{3,2,1,0:T(8,128)(2,1)}), bf16[32,2,32,256]{3,2,1,0:T(8,128)(2,1)}) %all-gather.7.cloned.1.call-update) | async-done | bytes 1048592 | tf_op jit(solution)/shard_map/all_gather | solution.py:74
  448.2 2.3 fusion.6
  450.5 6.5 copy.97
  457.0 7.8 %reshape.277 = bf16[8,2,32768]{2,1,0:T(2,128)(2,1)} reshape(bf16[256,2,32,32]{3,2,1,0:T(8,128)(2,1)} %bitcast.300) | data formatting | bytes 2097152
  464.8 4.8 all-to-all-start.2
  469.6 7.0 %reshape.280 = bf16[256,2,32,32]{3,2,1,0:T(8,128)(2,1)} reshape(bf16[8,2,32768]{2,1,0:T(2,128)(2,1)} %all-to-all-done.3) | data formatting | bytes 2097152
  476.6 6.7 %copy.104 = bf16[32,2,32,8,32]{2,3,4,1,0:T(8,128)(2,1)} copy(bf16[32,2,32,8,32]{0,2,1,4,3:T(8,128)(2,1)} %bitcast.305) | data formatting | bytes 2097152 | tf_op jit(solution)/shard_map/all_to_all | solution.py:80
  483.3 5.4 reshape.265
  488.7 3.4 fusion
  492.1 7.0 %reshape.278 = bf16[256,2,32,32]{3,2,1,0:T(8,128)(2,1)} reshape(bf16[8,2,32768]{2,1,0:T(2,128)(2,1)} %all-to-all-done.2) | data formatting | bytes 2097152
  499.1 6.7 %copy.98 = bf16[32,2,32,8,32]{2,3,4,1,0:T(8,128)(2,1)} copy(bf16[32,2,32,8,32]{0,2,1,4,3:T(8,128)(2,1)} %bitcast.307) | data formatting | bytes 2097152 | tf_op jit(solution)/shard_map/all_to_all | solution.py:80
  505.8 6.3 reshape.259
  512.1 6.2 multiply_reduce_fusion
  518.3 74.5 %all-reduce.1 = (f32[]{:T(128)}, f32[]{:T(128)}, f32[]{:T(128)}, f32[]{:T(128)}) all-reduce(f32[]{:T(128)} %get-tuple-element.20, f32[]{:T(128)} %get-tuple-element.16, f32[]{:T(128)} %get-tuple-element.15, f32[]{:T(128)} %get-tuple-element.19), channel_id=1, replica_groups=mesh['coil'=32,'slab'=8] {'coil','slab'}, use_global_device_ids=true, to_apply=%region_6.7 | all-reduce | flops 4 | bytes 32 | tf_op jit(solution)/shard_map/psum | solution.py:119
  595.3 2.1 fusion.12
  597.4 53.1 %all-gather = f32[64,32,32]{2,1,0:T(8,128)} all-gather(f32[2,32,32]{2,1,0:T(8,128)S(1)} %pad_maximum_fusion.7), channel_id=2, replica_groups=mesh['coil'=32,'slab'=8] {'coil'}, dimensions={0}, use_global_device_ids=true | all-gather | bytes 270336 | tf_op jit(solution)/shard_map/all_gather | solution.py:129
  655.8 2.3 fusion.14
  659.1 2.0 fusion.64
  (58 shorter events, 21.6 us)
Async XLA Ops:
  7.2 83.4 %all-gather.5.cloned.1.call-start = ((), (), s32[]{:S(2)}) async-start(), calls=%async_computation.4 | async-start | bytes 1081344 | tf_op jit(solution)/shard_map/all_gather | solution.py:74
  9.4 169.6 %all-gather.9.cloned.1.call-start = ((), (), s32[]{:S(2)}) async-start(), calls=%async_computation.6 | async-start | bytes 1081344 | tf_op jit(solution)/shard_map/all_gather | solution.py:74
  16.2 77.7 %copy-start.3 = (bf16[1,256,2,256]{3,1,0,2:T(8,128)(2,1)}, bf16[1,256,2,256]{3,1,0,2:T(8,128)(2,1)S(1)}, u32[]{:S(2)}) copy-start(bf16[1,256,2,256]{3,1,0,2:T(8,128)(2,1)S(1)} %get-tuple-element.47) | copy-start | bytes 786436
  112.1 6.5 copy-start.8
  112.2 6.6 copy-start.7
  112.2 20.0 %all-to-all-start = ((bf16[8,2,32768]{2,1,0:T(2,128)(2,1)}), bf16[8,2,32768]{2,1,0:T(2,128)(2,1)}, u32[]{:S(2)}, u32[]{:S(2)}) async-start(bf16[8,2,32768]{2,1,0:T(2,128)(2,1)} %reshape.273), calls=%async_computation | async-start | bytes 2097152 | tf_op jit(solution)/shard_map/all_to_all | solution.py:80
  152.0 4.4 copy-start.6
  173.2 20.2 %all-to-all-start.1 = ((bf16[8,2,32768]{2,1,0:T(2,128)(2,1)}), bf16[8,2,32768]{2,1,0:T(2,128)(2,1)}, u32[]{:S(2)}, u32[]{:S(2)}) async-start(bf16[8,2,32768]{2,1,0:T(2,128)(2,1)} %reshape.275), calls=%async_computation.1 | async-start | bytes 2097152 | tf_op jit(solution)/shard_map/all_to_all | solution.py:95
  178.7 189.4 %all-reduce.5.cloned.1.call-start = ((), (), s32[]{:S(2)}) async-start(), calls=%async_computation.7 | async-start | bytes 2097152
  213.4 2.2 copy-start.5
  215.6 1.6 copy-start.1
  219.2 1.7 copy-start.9
  219.2 148.9 %copy-start.4 = (f32[1,2,32,256]{3,2,1,0:T(8,128)S(1)}, f32[1,2,32,256]{3,2,1,0:T(8,128)}, u32[]{:S(2)}) copy-start(f32[1,2,32,256]{3,2,1,0:T(8,128)} %param.6) | copy-start | bytes 196612
  220.8 224.0 %all-gather.7.cloned.1.call-start = ((), (), s32[]{:S(2)}) async-start(), calls=%async_computation.5 | async-start | bytes 1081344 | tf_op jit(solution)/shard_map/all_gather | solution.py:74
  389.2 75.6 %all-to-all-start.3 = ((bf16[8,2,32768]{2,1,0:T(2,128)(2,1)}), bf16[8,2,32768]{2,1,0:T(2,128)(2,1)}, u32[]{:S(2)}, u32[]{:S(2)}) async-start(bf16[8,2,32768]{2,1,0:T(2,128)(2,1)} %reshape.279), calls=%async_computation.3 | async-start | bytes 2097152 | tf_op jit(solution)/shard_map/all_to_all | solution.py:80
  464.8 27.3 %all-to-all-start.2 = ((bf16[8,2,32768]{2,1,0:T(2,128)(2,1)}), bf16[8,2,32768]{2,1,0:T(2,128)(2,1)}, u32[]{:S(2)}, u32[]{:S(2)}) async-start(bf16[8,2,32768]{2,1,0:T(2,128)(2,1)} %reshape.277), calls=%async_computation.2 | async-start | bytes 2097152 | tf_op jit(solution)/shard_map/all_to_all | solution.py:80
  483.3 5.4 copy-start.2
  505.8 6.3 copy-start
Sparse Core Ops, SparseCore 0:
  11.1 79.3 all-gather.4
  93.1 73.8 all-gather.8
  221.0 147.1 all-reduce.4
  371.2 73.5 all-gather.6
